TPU v7x, 32 devices: a whole 2x2x4 slice. The times are simulated.
32 devices in a mesh: tm: 4 (over y, core), chan: 8 (over z, x).
Axes of the slice: x: 2, y: 2, z: 4, core: 2. Of those that a mesh axis runs over, the one named last changes fastest.
Arguments:
- traces: bfloat16 [8, 1024, 1024], P('tm', 'chan'), may hold values from -6 to 6
- lengths: int32 [8], replicated, may hold values from 512 to 1024
- source_blocks: int32 [3], replicated, may hold values from 0 to 31
Outputs:
- stacks: float32 [32, 3, 201, 1024], P('tm', None, None, 'chan')
Inputs may be any that keep to these rules, and one draw needn't show every extreme that they name: Step s takes the source channels 32 * source_blocks[s] to 32 * source_blocks[s] + 31. `lengths`: samples at and after a segment's length are not used.
All inputs are finite; a program needn't handle non-finite values.
Results may differ from a plain program's by a relative error of at most 0.0085.
Values may be sent and summed in bfloat16 or wider, within the bound.
No kernel may reach another device: no remote copies, remote signals or barrier semaphores. Data moves between devices by JAX's collectives and lax.ppermute only.
A program may use at most 256 MiB of HBM per device.

v0:
```python
import functools

import jax
import jax.numpy as jnp
from jax import lax
from jax.experimental import pallas as pl
from jax.experimental.pallas import tpu as pltpu
from jax.sharding import Mesh
from jax.sharding import PartitionSpec as P

MAXLAG = 100
SRC = 32
FINE = 16
LANES = 128
GROUP = 4
NEAR = 4
epsilon = 1e-06

SMEM = pl.BlockSpec(memory_space=pltpu.SMEM)
VMEM = pl.BlockSpec(memory_space=pltpu.VMEM)
HBM = pl.BlockSpec(memory_space=pltpu.HBM)
SMALL = pltpu.CompilerParams(vmem_limit_bytes=8 << 20)
WHOLE = pltpu.CompilerParams(vmem_limit_bytes=60 << 20)
LARGE = pltpu.CompilerParams(vmem_limit_bytes=20 << 20)


def plan(samp):
    half = samp // 2
    pairs = MAXLAG + 1
    blocks = -(-pairs // FINE)
    front = -(-(MAXLAG // 2) // FINE) * FINE
    base = front - MAXLAG // 2
    tail = -(-(base + FINE - 1) // FINE) * FINE
    rows = half + (blocks - 1) * FINE + tail
    full = pairs // FINE
    groups = [list(range(k, min(k + GROUP, full))) for k in range(0, full, GROUP)]
    groups += [[full]] if full < blocks else []
    return half, pairs, groups, front, base, tail, rows


def extract_kernel(per_owner, blocks_hbm, traces_ref, out_ref, owner_ref, first_ref, blocks_ref, buf, sems):
    steps = blocks_ref.shape[0]
    seg_dev, _, samp = traces_ref.shape
    _, rows, width = out_ref.shape
    share = rows // steps
    here = lax.axis_index("x")
    load = pltpu.make_async_copy(blocks_hbm, blocks_ref, sems.at[0])
    load.start()
    loads = []
    for n in range(seg_dev):
        copy = pltpu.make_async_copy(traces_ref.at[here ^ n], buf.at[n], sems.at[1 + n])
        copy.start()
        loads.append(copy)
    load.wait()
    for s in range(steps):
        owner_ref[s] = jnp.full(owner_ref.shape[1:], lax.div(blocks_ref[s], per_owner), jnp.int32)
    loads[0].wait()
    store = pltpu.make_async_copy(buf.at[0], first_ref, sems.at[1 + seg_dev])
    store.start()
    for copy in loads[1:]:
        copy.wait()
    for s in range(steps):
        first = pl.multiple_of(lax.rem(blocks_ref[s], per_owner) * SRC, SRC)
        for g in range(seg_dev):
            taken = buf[here ^ g, pl.ds(first, SRC), :]
            for q in range(SRC // share):
                for h in range(samp // width):
                    out_ref[(q * (samp // width) + h) * seg_dev + g, s * share:(s + 1) * share, :] = taken[
                        q * share:(q + 1) * share, h * width:(h + 1) * width
                    ]
    store.wait()


def extract(traces, source_blocks, n_tm):
    seg_dev, chans, samp = traces.shape
    steps = source_blocks.shape[0]
    share = SRC // n_tm
    return pl.pallas_call(
        functools.partial(extract_kernel, chans // SRC),
        out_shape=(
            jax.ShapeDtypeStruct((n_tm * 2 * seg_dev, steps * share, samp // 2), traces.dtype),
            jax.ShapeDtypeStruct((steps, share, LANES), jnp.int32),
            jax.ShapeDtypeStruct((chans, samp), traces.dtype),
        ),
        in_specs=[HBM, HBM],
        out_specs=(VMEM, VMEM, HBM),
        scratch_shapes=[
            pltpu.SMEM((steps,), jnp.int32),
            pltpu.VMEM((seg_dev, chans, samp), traces.dtype),
            pltpu.SemaphoreType.DMA((seg_dev + 2,)),
        ],
        compiler_params=WHOLE,
        name="extract",
    )(source_blocks, traces)


def pick_kernel(owner_ref, order_ref, got_ref, out_ref):
    steps, share, _ = owner_ref.shape
    n_tm, nsrc, width = out_ref.shape
    near = got_ref.shape[0] // n_tm
    rows_done = []
    for q in range(n_tm):
        for s in range(steps):
            rows = slice(s * share, (s + 1) * share)
            owner = owner_ref[s] & (near - 1)
            lanes = []
            for c in range(0, width, LANES):
                taken = got_ref[q * near, rows, c:c + LANES].astype(jnp.float32)
                for b in range(1, near):
                    other = got_ref[q * near + b, rows, c:c + LANES].astype(jnp.float32)
                    taken = jnp.where(owner == b, other, taken)
                lanes.append(taken)
            rows_done.append(jnp.concatenate(lanes, axis=1))
    taken = jnp.concatenate(rows_done, axis=0).astype(jnp.bfloat16)
    parted = jnp.dot(taken, order_ref[...], preferred_element_type=jnp.float32)
    for q in range(n_tm):
        out_ref[q] = parted[q * nsrc:(q + 1) * nsrc].astype(out_ref.dtype)


def pick(got, owners, order, n_tm):
    return pl.pallas_call(
        pick_kernel,
        out_shape=jax.ShapeDtypeStruct((n_tm,) + got.shape[1:], got.dtype),
        in_specs=[VMEM] * 3,
        out_specs=VMEM,
        compiler_params=SMALL,
        name="pick",
    )(owners, order, got)


def choose_kernel(bit, owner_ref, held_ref, came_ref, out_ref):
    steps, share, _ = owner_ref.shape
    n_tm, _, width = out_ref.shape
    here = lax.axis_index("zh") * NEAR
    for s in range(steps):
        rows = slice(s * share, (s + 1) * share)
        other = ((owner_ref[s] ^ here) & (bit * NEAR)) != 0
        for q in range(n_tm):
            for c in range(0, width, LANES):
                held = held_ref[q, rows, c:c + LANES].astype(jnp.float32)
                came = came_ref[q, rows, c:c + LANES].astype(jnp.float32)
                out_ref[q, rows, c:c + LANES] = jnp.where(other, came, held).astype(out_ref.dtype)


def choose(held, came, owners, bit):
    return pl.pallas_call(
        functools.partial(choose_kernel, bit),
        out_shape=jax.ShapeDtypeStruct(held.shape, held.dtype),
        in_specs=[VMEM, VMEM, VMEM],
        out_specs=VMEM,
        compiler_params=SMALL,
        name="choose",
    )(owners, held, came)


def whitened(block, count, work):
    xt = block.T.astype(jnp.float32)
    half = xt.shape[0] // 2
    pos = lax.broadcasted_iota(jnp.int32, xt.shape, 0)
    xt = jnp.where(pos < count, xt, 0.0)
    power = jnp.sum(xt * xt, axis=0, keepdims=True) / jnp.asarray(count).astype(jnp.float32)
    work[0:2 * half, :] = xt * (1.0 / jnp.sqrt(power + epsilon))
    return (
        work[pl.ds(0, half, stride=2), :].astype(jnp.bfloat16),
        work[pl.ds(1, half, stride=2), :].astype(jnp.bfloat16),
    )


def pad_into(ref, even, odd, work):
    half, chans = even.shape
    _, _, _, front, _, _, rows = plan(2 * half)
    even = even.astype(jnp.float32)
    wide = odd.astype(jnp.float32)
    work[0:half, :] = even
    work[half:half + 8, :] = jnp.zeros((8, chans), jnp.float32)
    after = work[1:half + 1, :]
    ref[0, front:front + half, :] = (even - wide).astype(ref.dtype)
    ref[1, front:front + half, :] = odd
    ref[2, front:front + half, :] = (after - wide).astype(ref.dtype)
    row = lax.broadcasted_iota(jnp.int32, (FINE, chans), 0)
    last = jnp.where(row == FINE - 1, jnp.broadcast_to(work[0:1, :], (FINE, chans)), 0.0)
    for n in range(3):
        ref[n, 0:front, :] = jnp.zeros((front, chans), ref.dtype)
        ref[n, front + half:rows, :] = jnp.zeros((rows - front - half, chans), ref.dtype)
    ref[2, front - FINE:front, :] = last.astype(ref.dtype)


def prepare_here_kernel(
    len_ref, traces_ref, owner_ref, first_ref, second_ref, bare_ref, passed_ref, order_ref, count_ref, work
):
    seg_dev = traces_ref.shape[0]
    for n in range(len_ref.shape[0]):
        count_ref[n:n + 1, :] = jnp.full((1, count_ref.shape[1]), len_ref[n], jnp.int32)
    passed_ref[...] = owner_ref[...]
    width = order_ref.shape[0]
    source = lax.broadcasted_iota(jnp.int32, (width, width), 0)
    place = lax.broadcasted_iota(jnp.int32, (width, width), 1)
    wanted = jnp.where(place < width // 2, 2 * place, 2 * place - width + 1)
    order_ref[...] = (source == wanted).astype(jnp.float32).astype(order_ref.dtype)
    here = lax.axis_index("x")
    row = lax.axis_index("tm") * seg_dev
    even, odd = whitened(traces_ref[here], len_ref[row + here], work)
    pad_into(first_ref, even, odd, work)
    even, odd = whitened(traces_ref[here ^ 1], len_ref[row + (here ^ 1)], work)
    bare_ref[0] = even
    bare_ref[1] = odd
    pad_into(second_ref, even, odd, work)


def prepare_here(traces, owners, lengths):
    _, chans, samp = traces.shape
    half = samp // 2
    full = jax.ShapeDtypeStruct((3, plan(samp)[-1], chans), jnp.bfloat16)
    bare = jax.ShapeDtypeStruct((2, half, chans), jnp.bfloat16)
    return pl.pallas_call(
        prepare_here_kernel,
        out_shape=(
            full,
            full,
            bare,
            jax.ShapeDtypeStruct(owners.shape, owners.dtype),
            jax.ShapeDtypeStruct((half, half), jnp.bfloat16),
            jax.ShapeDtypeStruct((lengths.shape[0], LANES), jnp.int32),
        ),
        in_specs=[SMEM, VMEM, VMEM],
        out_specs=(VMEM,) * 6,
        scratch_shapes=[pltpu.VMEM((samp + FINE, chans), jnp.float32)],
        compiler_params=SMALL,
        cost_estimate=pl.CostEstimate(flops=0, bytes_accessed=4 << 20, transcendentals=0),
        name="prepare_here",
    )(lengths, traces, owners)


def prepare_there_kernel(distances, seg_dev, count_ref, *refs):
    count_parts = len(distances)
    work = refs[-1]
    for distance, part_ref, out_ref in zip(distances, refs[:count_parts], refs[count_parts:-1]):
        seg = (lax.axis_index("tm") ^ distance) * seg_dev + lax.axis_index("x")
        even, odd = whitened(part_ref[...], count_ref[pl.ds(seg, 1), 0:part_ref.shape[0]], work)
        pad_into(out_ref, even, odd, work)


def prepare_there(named, seg_dev, counts):
    chans, samp = next(iter(named.values())).shape
    full = jax.ShapeDtypeStruct((3, plan(samp)[-1], chans), jnp.bfloat16)
    done = pl.pallas_call(
        functools.partial(prepare_there_kernel, tuple(named), seg_dev),
        out_shape=(full,) * len(named),
        in_specs=[VMEM] * (1 + len(named)),
        out_specs=(VMEM,) * len(named),
        scratch_shapes=[pltpu.VMEM((samp + FINE, chans), jnp.float32)],
        compiler_params=SMALL,
        cost_estimate=pl.CostEstimate(
            flops=0, bytes_accessed=len(named) << 21, transcendentals=0
        ),
        name="prepare_there",
    )(counts, *named.values())
    return dict(zip(named, done))


def correlate_kernel(n_parts, flip, first, steps, count_ref, near_ref, far_ref, *refs):
    parts = list(refs[:n_parts])
    (pads, work), refs = refs[-2:], refs[:-2]
    if first:
        out_ref, lhs, tailbuf = refs[n_parts:]
        carry_ref = None
    else:
        carry_ref, out_ref, buf, lhs, tailbuf, sems = refs[n_parts:]
    seg_dev = count_ref.shape[0] // n_parts
    chans = parts[0].shape[-1]
    _, nsrc, width = near_ref.shape
    share = nsrc // steps
    half, pairs, groups, front, base, tail, _ = plan(2 * width)
    quarter = width // 2
    bf = jnp.bfloat16
    tm_here = lax.axis_index("tm")
    local = lax.axis_index("x") ^ flip
    low_here = lax.axis_index("zl") == 0

    def build(m):
        if parts[m].shape[0] == 2:
            pad_into(pads.at[m], parts[m][0], parts[m][1], work)
            parts[m] = pads.at[m]
        q = tm_here ^ m
        count = count_ref[pl.ds(q * seg_dev + local, 1), 0:1]
        countf = count.astype(jnp.float32)
        near = near_ref[q].astype(jnp.float32)
        far = far_ref[q].astype(jnp.float32)
        low, high = jnp.where(low_here, near, far), jnp.where(low_here, far, near)
        sides = []
        for parity in range(2):
            x = jnp.concatenate(
                [low[:, parity * quarter:(parity + 1) * quarter], high[:, parity * quarter:(parity + 1) * quarter]],
                axis=1,
            )
            pos = 2 * lax.broadcasted_iota(jnp.int32, x.shape, 1) + parity
            sides.append(jnp.where(pos < count, x, 0.0))
        even, odd = sides
        power = jnp.sum(even * even + odd * odd, axis=1, keepdims=True) / countf
        scale = 1.0 / (jnp.sqrt(power + epsilon) * jnp.sqrt(countf))
        even, odd = even * scale, odd * scale
        for n, x in enumerate((even, even + odd, odd)):
            x = jnp.concatenate([x, jnp.zeros((nsrc, LANES), jnp.float32)], axis=1)
            for s in range(steps):
                rowsx = x[s * share:(s + 1) * share]
                for r in range(0, FINE, 2):
                    t = jnp.concatenate(
                        [pltpu.roll(rowsx, base + r + d, 1) for d in range(2)], axis=0
                    )
                    at = slice((s * FINE + r) * share, (s * FINE + r + 2) * share)
                    lhs[n, at, m * half:(m + 1) * half] = t[:, :half].astype(bf)
                    last = t[:, half:]
                    if m:
                        last = tailbuf[n, at, :] + pltpu.roll(last, m * tail, 1)
                    if m == n_parts - 1:
                        lhs[n, at, n_parts * half:] = last.astype(bf)
                    else:
                        tailbuf[n, at, :] = last

    copies = []
    for group, ks in enumerate(groups):
        used = min(FINE, pairs - ks[0] * FINE)

        def window(m, n, start, size):
            return jnp.concatenate(
                [parts[m][n, start + k * FINE:start + k * FINE + size, :] for k in ks], axis=1
            )

        def shifted(n, lo, hi):
            if used == FINE:
                return lhs[n, :, lo:hi]
            return jnp.concatenate(
                [lhs[n, s * FINE * share:(s * FINE + used) * share, lo:hi] for s in range(steps)], axis=0
            )

        sums = []
        for n in range(3):
            total = None
            for m in range(n_parts):
                if not group and not n:
                    build(m)
                term = jnp.dot(
                    shifted(n, m * half, (m + 1) * half),
                    window(m, n, 0, half),
                    preferred_element_type=jnp.float32,
                )
                total = term if total is None else total + term
            if ks[0] * FINE < front:
                ends = jnp.concatenate([window(m, n, half, tail) for m in range(n_parts)], axis=0)
                total = total + jnp.dot(
                    shifted(n, n_parts * half, n_parts * (half + tail)), ends, preferred_element_type=jnp.float32
                )
            sums.append(total)
        across = len(ks) * chans
        both = [sums[0] + sums[1], sums[1] + sums[2]]
        height = both[0].shape[0]
        for parity in range(2):
            if first:
                out_ref[group, parity, 0:height, 0:across] = both[parity]
                continue
            acc = both[parity] + carry_ref[group, parity, 0:height, 0:across]
            for p, k in enumerate(ks):
                for s in range(steps):
                    for r in range(used):
                        lag = 2 * (k * FINE + r) + parity
                        if lag <= 2 * MAXLAG:
                            at = (s * used + r) * share
                            buf[s, lag] = acc[at:at + share, p * chans:(p + 1) * chans]
        if not first:
            lag0, lag1 = 2 * ks[0] * FINE, min(2 * (ks[-1] + 1) * FINE, 2 * MAXLAG + 1)
            copy = pltpu.make_async_copy(
                buf.at[:, lag0:lag1], out_ref.at[:, lag0:lag1], sems.at[group]
            )
            copy.start()
            copies.append(copy)
    for copy in copies:
        copy.wait()


def correlate(parts, near, far, counts, steps, flip, carry=None):
    chans = parts[0].shape[-1]
    _, nsrc, width = near.shape
    samp = 2 * width
    n_parts = len(parts)
    half, pairs, groups, _, _, tail, rows = plan(samp)
    ends = -(-n_parts * tail // LANES) * LANES
    first = carry is None
    work = [
        pltpu.VMEM((3, nsrc * FINE, n_parts * half + ends), jnp.bfloat16),
        pltpu.VMEM((3, nsrc * FINE, LANES), jnp.float32),
    ]
    if first:
        shape = (len(groups), 2, nsrc * FINE, GROUP * chans)
    else:
        shape = (steps, 2 * MAXLAG + 1, nsrc // steps, chans)
        work = [pltpu.VMEM(shape, jnp.float32)] + work + [pltpu.SemaphoreType.DMA((len(groups),))]
    work.append(pltpu.VMEM((n_parts, 3, rows, chans), jnp.bfloat16))
    work.append(pltpu.VMEM((samp + FINE, chans), jnp.float32))
    return pl.pallas_call(
        functools.partial(correlate_kernel, n_parts, flip, first, steps),
        out_shape=jax.ShapeDtypeStruct(shape, jnp.float32),
        in_specs=[VMEM] * (3 + n_parts) + ([] if first else [VMEM]),
        out_specs=VMEM if first else HBM,
        scratch_shapes=work,
        compiler_params=LARGE,
        cost_estimate=pl.CostEstimate(
            flops=3 * nsrc * pairs * chans * samp * n_parts, bytes_accessed=8 << 20, transcendentals=0
        ),
        name="correlate",
    )(counts, near, far, *parts, *([] if first else [carry]))


def swap(value, axis, size, distance):
    return lax.ppermute(value, axis, [(i, i ^ distance) for i in range(size)])


def shards(n_tm, n_far, traces, lengths, source_blocks):
    seg_dev = traces.shape[0]
    steps = source_blocks.shape[0]
    sent, owners, own = extract(traces, source_blocks, n_tm)
    got = lax.all_to_all(sent, ("tm", "zl", "x"), 0, 0)
    first, second, bare, owners, order, counts = prepare_here(traces, owners, lengths)
    held = pick(got, owners, order, n_tm)
    bit = 1
    while bit < n_far:
        came = swap(held, "zh", n_far, bit)
        held = choose(held, came, owners, bit)
        bit *= 2
    near = held
    far = swap(near, "zl", 2, 1)
    near_x = swap(near, "x", 2, 1)
    far_x = lax.ppermute(near, ("zl", "x"), [(i, i ^ 3) for i in range(NEAR)])
    firsts, seconds = {0: first}, {0: second}
    raw, bares = {0: own}, {0: bare}
    top = n_tm // 2
    bit = top
    while bit:
        for m in sorted(set(raw) | set(firsts)):
            if m | bit < top:
                firsts[m | bit] = swap(firsts[m], "tm", n_tm, bit)
            else:
                raw[m | bit] = swap(raw[m], "tm", n_tm, bit)
            if m | bit < top:
                seconds[m | bit] = swap(seconds[m], "tm", n_tm, bit)
            else:
                bares[m | bit] = swap(bares[m], "tm", n_tm, bit)
        bit //= 2
    firsts.update(prepare_there({m: raw[m] for m in raw if m}, seg_dev, counts))
    for m in bares:
        if m:
            seconds[m] = bares[m]
    carry = correlate([firsts[m] for m in range(n_tm)], near, far, counts, steps, 0)
    out = correlate([seconds[m] for m in range(n_tm)], near_x, far_x, counts, steps, 1, carry)
    return jnp.transpose(out, (2, 0, 1, 3))


def solution(mesh):
    n_tm, n_chan = mesh.shape["tm"], mesh.shape["chan"]
    split = Mesh(
        mesh.devices.reshape(n_tm, n_chan // NEAR, 2, 2), ("tm", "zh", "zl", "x")
    )
    chan = ("zh", "zl", "x")
    return jax.shard_map(
        functools.partial(shards, n_tm, n_chan // NEAR),
        mesh=split,
        in_specs=(P("tm", chan, None), P(), P()),
        out_specs=P("tm", None, None, chan),
        check_vma=False,
    )
```

profile of v0, /device:TPU:0, one launch (start us, length us, event | category | flops | bytes accessed | tf_op | source)
XLA Modules:
  0.0 47.7 jit_solution(12711918144139618923)
XLA Ops:
  0.0 2.4 %extract.1 = (bf16[16,24,512]{2,1,0:T(8,128)(2,1)}, s32[3,8,128]{2,1,0:T(8,128)}, bf16[128,1024]{1,0:T(8,128)(2,1)}) custom-call(s32[3]{0:T(128)} %blocks_hbm.1, bf16[2,128,1024]{2,1,0:T(8,128)(2,1)} %traces_ref.3), custom_call_target="tpu_custom_call" | custom-call | tf_op jit(solution)/shard_map/extract/pallas_call | solution.py:78
  2.4 6.3 %all-to-all-start = ((bf16[16,24,512]{2,1,0:T(8,128)(2,1)}), bf16[16,24,512]{2,1,0:T(8,128)(2,1)S(1)}, u32[]{:S(2)}, u32[]{:S(2)}) async-start(bf16[16,24,512]{2,1,0:T(8,128)(2,1)} %get-tuple-element.20), calls=%async_computation | async-start | bytes 786432 | tf_op jit(solution)/shard_map/all_to_all | solution.py:421
  8.8 1.9 %collective-permute-start.8 = (bf16[128,1024]{1,0:T(8,128)(2,1)}, bf16[128,1024]{1,0:T(8,128)(2,1)S(1)}, u32[]{:S(2)}, u32[]{:S(2)}) collective-permute-start(bf16[128,1024]{1,0:T(8,128)(2,1)} %get-tuple-element.24), channel_id=1, source_target_pairs={{0,16},{8,24},{16,0},{24,8},{1,17},{9,25},{17,1},{25,9},{2,18},{10... | collective-permute-start | bytes 786440 | tf_op jit(solution)/shard_map/ppermute | solution.py:414
  10.7 0.0 copy-start
  10.7 1.0 %copy-done = bf16[2,128,1024]{2,1,0:T(8,128)(2,1)S(1)} copy-done((bf16[2,128,1024]{2,1,0:T(8,128)(2,1)S(1)}, bf16[2,128,1024]{2,1,0:T(8,128)(2,1)}, u32[]{:S(2)}) %copy-start) | copy-done | bytes 524312
  11.7 0.0 copy-start.1
  11.7 0.7 %copy-done.1 = s32[3,8,128]{2,1,0:T(8,128)S(1)} copy-done((s32[3,8,128]{2,1,0:T(8,128)S(1)}, s32[3,8,128]{2,1,0:T(8,128)}, u32[]{:S(2)}) %copy-start.1) | copy-done | bytes 12312
  12.4 0.0 copy-start.2
  12.4 0.7 %copy-done.2 = s32[8]{0:T(128)S(1)} copy-done((s32[8]{0:T(128)S(1)}, s32[8]{0:T(128)}, u32[]{:S(2)}) %copy-start.2) | copy-done | bytes 56
  13.1 1.2 %prepare_here.1 = (bf16[3,640,128]{2,1,0:T(8,128)(2,1)S(1)}, bf16[3,640,128]{2,1,0:T(8,128)(2,1)S(1)}, bf16[2,512,128]{2,1,0:T(8,128)(2,1)S(1)}, s32[3,8,128]{2,...) custom-call(s32[8]{0:T(128)S(1)} %copy-done.2, bf16[2,128,1024]{2,1,0:T(8,128)(2,1)S(1)} %copy-done, ...), custom_call_target="tpu_custom_call" | custom-call | bytes 4194304 | tf_op jit(solution)/shard_map/prepare_here/pallas_call | solution.py:215
  14.3 0.1 collective-permute-start.7
  14.4 0.2 collective-permute-start.4
  14.6 7.6 %collective-permute-done.8.refs_0_ = bf16[128,1024]{1,0:T(8,128)(2,1)S(1)} collective-permute-done((bf16[128,1024]{1,0:T(8,128)(2,1)}, bf16[128,1024]{1,0:T(8,128)(2,1)S(1)}, u32[]{:S(2)}, u32[]{:S(2)}) %collective-permute-start.8) | collective-permute-done | bytes 262176 | tf_op jit(solution)/shard_map/ppermute | solution.py:414
  22.3 0.0 collective-permute-start.9
  22.3 0.0 all-to-all-done.got_ref
  22.3 0.2 pick.1.held_ref
  22.5 2.7 %collective-permute-start = (bf16[4,24,512]{2,1,0:T(8,128)(2,1)S(1)}, bf16[4,24,512]{2,1,0:T(8,128)(2,1)S(1)}, u32[]{:S(2)}, u32[]{:S(2)}) collective-permute-start(bf16[4,24,512]{2,1,0:T(8,128)(2,1)S(1)} %pick.1.held_ref), channel_id=1, source_target_pairs={{0,4},{4,0},{1,5},{5,1},{2,6},{6,2},{3,7},{7,3},{8,12},{12,8},{9,1... | collective-permute-start | bytes 294920 | tf_op jit(solution)/shard_map/ppermute | solution.py:414
  25.1 0.2 collective-permute-start.3
  25.4 5.4 %collective-permute-done.came_ref = bf16[4,24,512]{2,1,0:T(8,128)(2,1)S(1)} collective-permute-done((bf16[4,24,512]{2,1,0:T(8,128)(2,1)S(1)}, bf16[4,24,512]{2,1,0:T(8,128)(2,1)S(1)}, u32[]{:S(2)}, u32[]{:S(2)}) %collective-permute-start) | collective-permute-done | bytes 98336 | tf_op jit(solution)/shard_map/ppermute | solution.py:414
  30.8 0.2 collective-permute-start.6
  31.0 0.0 collective-permute-done.4.refs_2_
  31.0 0.0 collective-permute-start.5
  31.0 0.0 collective-permute-done.9.refs_1_
  31.0 0.6 %prepare_there.1 = (bf16[3,640,128]{2,1,0:T(8,128)(2,1)S(1)}, bf16[3,640,128]{2,1,0:T(8,128)(2,1)S(1)}) custom-call(s32[8,128]{1,0:T(8,128)S(1)} %get-tuple-element.17.count_ref, bf16[128,1024]{1,0:T(8,128)(2,1)S(1)} %collective-permute-done.8.refs_0_, bf16[128,1024]{1,0:T(8,128)(2,1)S(1)} %collective-permute-done.9.refs_1_), custom_call_target="tpu_custom_call" | custom-call | bytes 4194304 | tf_op jit(solution)/shard_map/prepare_there/pallas_call | solution.py:246
  31.7 2.6 %collective-permute-start.2 = (bf16[4,24,512]{2,1,0:T(8,128)(2,1)S(1)}, bf16[4,24,512]{2,1,0:T(8,128)(2,1)S(1)}, u32[]{:S(2)}, u32[]{:S(2)}) collective-permute-start(bf16[4,24,512]{2,1,0:T(8,128)(2,1)S(1)} %choose.1.near_ref), channel_id=1, source_target_pairs={{0,3},{1,2},{2,1},{3,0},{4,7},{5,6},{6,5},{7,4},{8,11},{9,10},{10,... | collective-permute-start | bytes 294920 | tf_op jit(solution)/shard_map/ppermute | solution.py:432
  34.3 0.0 collective-permute-done.7.refs_1_
  34.3 0.8 %collective-permute-start.1 = (bf16[4,24,512]{2,1,0:T(8,128)(2,1)S(1)}, bf16[4,24,512]{2,1,0:T(8,128)(2,1)S(1)}, u32[]{:S(2)}, u32[]{:S(2)}) collective-permute-start(bf16[4,24,512]{2,1,0:T(8,128)(2,1)S(1)} %choose.1.near_ref), channel_id=1, source_target_pairs={{0,1},{1,0},{2,3},{3,2},{4,5},{5,4},{6,7},{7,6},{8,9},{9,8},{10,11... | collective-permute-start | bytes 294920 | tf_op jit(solution)/shard_map/ppermute | solution.py:414
  35.1 0.4 collective-permute-done.6.far_ref
  35.5 5.6 %correlate.2.refs_4_ = f32[3,2,384,512]{3,2,1,0:T(8,128)S(1)} custom-call(s32[8,128]{1,0:T(8,128)S(1)} %get-tuple-element.17.count_ref, bf16[4,24,512]{2,1,0:T(8,128)(2,1)S(1)} %choose.1.near_ref, bf16[4,24,512]{2,1,0:T(8,128)(2,1)S(1)} %collective-permute-done.6.far_ref, bf16[3,640,128]{2,1,0:T(8,128)(2,1)S(1)} %get-tuple-element.23.refs_0_, ...), custom_call_target="tpu_custom_call" | custom-call | flops 3812622336 | bytes 8388608 | tf_op jit(solution)/shard_map/correlate/pallas_call | solution.py:399
  41.1 0.0 collective-permute-done.3.refs_1_
  41.1 0.0 collective-permute-done.5.refs_3_
  41.1 0.0 collective-permute-done.2.far_ref
  41.1 0.0 collective-permute-done.1.near_ref
  41.1 6.6 %correlate.3 = f32[3,201,8,128]{3,2,1,0:T(8,128)} custom-call(s32[8,128]{1,0:T(8,128)S(1)} %get-tuple-element.17.count_ref, bf16[4,24,512]{2,1,0:T(8,128)(2,1)S(1)} %collective-permute-done.1.near_ref, bf16[4,24,512]{2,1,0:T(8,128)(2,1)S(1)} %collective-permute-done.2.far_ref, bf16[3,640,128]{2,1,0:T(8,128)(2,1)S(1)} %get-tuple-element.21.refs_0_, ...), custom_call_target="tpu_custom_call" | custom-call | flops 3812622336 | bytes 8388608 | tf_op jit(solution)/shard_map/correlate/pallas_call | solution.py:399
  (1 shorter events, 0.0 us)
Async XLA Ops:
  2.4 19.8 %all-to-all-start = ((bf16[16,24,512]{2,1,0:T(8,128)(2,1)}), bf16[16,24,512]{2,1,0:T(8,128)(2,1)S(1)}, u32[]{:S(2)}, u32[]{:S(2)}) async-start(bf16[16,24,512]{2,1,0:T(8,128)(2,1)} %get-tuple-element.20), calls=%async_computation | async-start | bytes 786432 | tf_op jit(solution)/shard_map/all_to_all | solution.py:421
  8.8 13.5 %collective-permute-start.8 = (bf16[128,1024]{1,0:T(8,128)(2,1)}, bf16[128,1024]{1,0:T(8,128)(2,1)S(1)}, u32[]{:S(2)}, u32[]{:S(2)}) collective-permute-start(bf16[128,1024]{1,0:T(8,128)(2,1)} %get-tuple-element.24), channel_id=1, source_target_pairs={{0,16},{8,24},{16,0},{24,8},{1,17},{9,25},{17,1},{25,9},{2,18},{10... | collective-permute-start | bytes 786440 | tf_op jit(solution)/shard_map/ppermute | solution.py:414
  10.7 1.0 %copy-start = (bf16[2,128,1024]{2,1,0:T(8,128)(2,1)S(1)}, bf16[2,128,1024]{2,1,0:T(8,128)(2,1)}, u32[]{:S(2)}) copy-start(bf16[2,128,1024]{2,1,0:T(8,128)(2,1)} %traces_ref.3) | copy-start | bytes 1572868
  11.7 0.7 %copy-start.1 = (s32[3,8,128]{2,1,0:T(8,128)S(1)}, s32[3,8,128]{2,1,0:T(8,128)}, u32[]{:S(2)}) copy-start(s32[3,8,128]{2,1,0:T(8,128)} %get-tuple-element.16.owner_ref) | copy-start | bytes 36868
  12.4 0.7 %copy-start.2 = (s32[8]{0:T(128)S(1)}, s32[8]{0:T(128)}, u32[]{:S(2)}) copy-start(s32[8]{0:T(128)} %len_ref.1) | copy-start | bytes 100
  14.3 20.0 %collective-permute-start.7 = (bf16[3,640,128]{2,1,0:T(8,128)(2,1)S(1)}, bf16[3,640,128]{2,1,0:T(8,128)(2,1)S(1)}, u32[]{:S(2)}, u32[]{:S(2)}) collective-permute-start(bf16[3,640,128]{2,1,0:T(8,128)(2,1)S(1)} %get-tuple-element.23.refs_0_), channel_id=1, source_target_pairs={{0,8},{8,0},{16,24},{24,16},{1,9},{9,1},{17,25},{25,17},{2,10},{10... | collective-permute-start | bytes 1474568 | tf_op jit(solution)/shard_map/ppermute | solution.py:414
  14.4 16.6 %collective-permute-start.4 = (bf16[2,512,128]{2,1,0:T(8,128)(2,1)S(1)}, bf16[2,512,128]{2,1,0:T(8,128)(2,1)S(1)}, u32[]{:S(2)}, u32[]{:S(2)}) collective-permute-start(bf16[2,512,128]{2,1,0:T(8,128)(2,1)S(1)} %get-tuple-element.22), channel_id=1, source_target_pairs={{0,16},{8,24},{16,0},{24,8},{1,17},{9,25},{17,1},{25,9},{2,18},{10... | collective-permute-start | bytes 786440 | tf_op jit(solution)/shard_map/ppermute | solution.py:414
  22.3 8.8 %collective-permute-start.9 = (bf16[128,1024]{1,0:T(8,128)(2,1)S(1)}, bf16[128,1024]{1,0:T(8,128)(2,1)S(1)}, u32[]{:S(2)}, u32[]{:S(2)}) collective-permute-start(bf16[128,1024]{1,0:T(8,128)(2,1)S(1)} %collective-permute-done.8.refs_0_), channel_id=1, source_target_pairs={{0,8},{8,0},{16,24},{24,16},{1,9},{9,1},{17,25},{25,17},{2,10},{10... | collective-permute-start | bytes 786440 | tf_op jit(solution)/shard_map/ppermute | solution.py:414
  22.5 8.3 %collective-permute-start = (bf16[4,24,512]{2,1,0:T(8,128)(2,1)S(1)}, bf16[4,24,512]{2,1,0:T(8,128)(2,1)S(1)}, u32[]{:S(2)}, u32[]{:S(2)}) collective-permute-start(bf16[4,24,512]{2,1,0:T(8,128)(2,1)S(1)} %pick.1.held_ref), channel_id=1, source_target_pairs={{0,4},{4,0},{1,5},{5,1},{2,6},{6,2},{3,7},{7,3},{8,12},{12,8},{9,1... | collective-permute-start | bytes 294920 | tf_op jit(solution)/shard_map/ppermute | solution.py:414
  25.1 15.9 %collective-permute-start.3 = (bf16[3,640,128]{2,1,0:T(8,128)(2,1)S(1)}, bf16[3,640,128]{2,1,0:T(8,128)(2,1)S(1)}, u32[]{:S(2)}, u32[]{:S(2)}) collective-permute-start(bf16[3,640,128]{2,1,0:T(8,128)(2,1)S(1)} %get-tuple-element.21.refs_0_), channel_id=1, source_target_pairs={{0,8},{8,0},{16,24},{24,16},{1,9},{9,1},{17,25},{25,17},{2,10},{10... | collective-permute-start | bytes 1474568 | tf_op jit(solution)/shard_map/ppermute | solution.py:414
  30.8 4.7 %collective-permute-start.6 = (bf16[4,24,512]{2,1,0:T(8,128)(2,1)S(1)}, bf16[4,24,512]{2,1,0:T(8,128)(2,1)S(1)}, u32[]{:S(2)}, u32[]{:S(2)}) collective-permute-start(bf16[4,24,512]{2,1,0:T(8,128)(2,1)S(1)} %choose.1.near_ref), channel_id=1, source_target_pairs={{0,2},{2,0},{1,3},{3,1},{4,6},{6,4},{5,7},{7,5},{8,10},{10,8},{9,1... | collective-permute-start | bytes 294920 | tf_op jit(solution)/shard_map/ppermute | solution.py:414
  31.0 10.1 %collective-permute-start.5 = (bf16[2,512,128]{2,1,0:T(8,128)(2,1)S(1)}, bf16[2,512,128]{2,1,0:T(8,128)(2,1)S(1)}, u32[]{:S(2)}, u32[]{:S(2)}) collective-permute-start(bf16[2,512,128]{2,1,0:T(8,128)(2,1)S(1)} %collective-permute-done.4.refs_2_), channel_id=1, source_target_pairs={{0,8},{8,0},{16,24},{24,16},{1,9},{9,1},{17,25},{25,17},{2,10},{10... | collective-permute-start | bytes 786440 | tf_op jit(solution)/shard_map/ppermute | solution.py:414
  31.7 9.4 %collective-permute-start.2 = (bf16[4,24,512]{2,1,0:T(8,128)(2,1)S(1)}, bf16[4,24,512]{2,1,0:T(8,128)(2,1)S(1)}, u32[]{:S(2)}, u32[]{:S(2)}) collective-permute-start(bf16[4,24,512]{2,1,0:T(8,128)(2,1)S(1)} %choose.1.near_ref), channel_id=1, source_target_pairs={{0,3},{1,2},{2,1},{3,0},{4,7},{5,6},{6,5},{7,4},{8,11},{9,10},{10,... | collective-permute-start | bytes 294920 | tf_op jit(solution)/shard_map/ppermute | solution.py:432
  34.3 6.8 %collective-permute-start.1 = (bf16[4,24,512]{2,1,0:T(8,128)(2,1)S(1)}, bf16[4,24,512]{2,1,0:T(8,128)(2,1)S(1)}, u32[]{:S(2)}, u32[]{:S(2)}) collective-permute-start(bf16[4,24,512]{2,1,0:T(8,128)(2,1)S(1)} %choose.1.near_ref), channel_id=1, source_target_pairs={{0,1},{1,0},{2,3},{3,2},{4,5},{5,4},{6,7},{7,6},{8,9},{9,8},{10,11... | collective-permute-start | bytes 294920 | tf_op jit(solution)/shard_map/ppermute | solution.py:414
where the time goes:
time: 48.1 us; the launch traced here: 47.7 us
  Pallas kernels  16.7 us (35%)
  starting transfers between devices  15.1 us (31%)
  waiting for transfers between devices  13.5 us (28%)
  local copies, waits for them, and re-layouts  2.4 us (5%)
    ppermute x9, waiting for transfers between devices, swap(): return lax.ppermute(value, axis, [(i, i ^ distance) for i in range(size)])  13.5 us
    pallas_call x2, Pallas kernels, correlate(): pl.pallas_call(functools.partial(correlate_kernel, n_parts, flip, first,...  12.2 us
    all_to_all x1, starting transfers between devices, shards(): got = lax.all_to_all(sent, ('tm', 'zl', 'x'), 0, 0)  6.33 us
    ppermute x9, starting transfers between devices, swap(): return lax.ppermute(value, axis, [(i, i ^ distance) for i in range(size)])  6.1 us
    ppermute x1, starting transfers between devices, shards(): far_x = lax.ppermute(near, ('zl', 'x'), [(i, i ^ 3) for i in range(NEAR)])  2.63 us
    pallas_call x1, Pallas kernels, extract(): pl.pallas_call(functools.partial(extract_kernel, chans // SRC), out_shape...  2.42 us
    unnamed x6, local copies, waits for them, and re-layouts  2.4 us
    pallas_call x1, Pallas kernels, prepare_here(): pl.pallas_call(prepare_here_kernel, out_shape=(full, full, bare, jax.Shap...  1.2 us
  transfers between devices with their start and end apart: 11, of which 3 were waited for; matrix products, arithmetic and copies ran while one was open for 0% of the time, Pallas kernels for 16%

commit v1 on v0

--- a/solution.py
+++ b/solution.py
@@ -65,7 +65,7 @@
             taken = buf[here ^ g, pl.ds(first, SRC), :]
             for q in range(SRC // share):
                 for h in range(samp // width):
-                    out_ref[(q * (samp // width) + h) * seg_dev + g, s * share:(s + 1) * share, :] = taken[
+                    out_ref[(q * seg_dev + g) * (samp // width) + h, s * share:(s + 1) * share, :] = taken[
                         q * share:(q + 1) * share, h * width:(h + 1) * width
                     ]
     store.wait()
@@ -418,7 +418,7 @@
     seg_dev = traces.shape[0]
     steps = source_blocks.shape[0]
     sent, owners, own = extract(traces, source_blocks, n_tm)
-    got = lax.all_to_all(sent, ("tm", "zl", "x"), 0, 0)
+    got = lax.all_to_all(sent, ("tm", "x", "zl"), 0, 0)
     first, second, bare, owners, order, counts = prepare_here(traces, owners, lengths)
     held = pick(got, owners, order, n_tm)
     bit = 1
@@ -429,7 +429,7 @@
     near = held
     far = swap(near, "zl", 2, 1)
     near_x = swap(near, "x", 2, 1)
-    far_x = lax.ppermute(near, ("zl", "x"), [(i, i ^ 3) for i in range(NEAR)])
+    far_x = swap(far, "x", 2, 1)
     firsts, seconds = {0: first}, {0: second}
     raw, bares = {0: own}, {0: bare}
     top = n_tm // 2
@@ -457,9 +457,9 @@
 def solution(mesh):
     n_tm, n_chan = mesh.shape["tm"], mesh.shape["chan"]
     split = Mesh(
-        mesh.devices.reshape(n_tm, n_chan // NEAR, 2, 2), ("tm", "zh", "zl", "x")
+        mesh.devices.reshape(n_tm, n_chan // NEAR, 2, 2), ("tm", "zh", "x", "zl")
     )
-    chan = ("zh", "zl", "x")
+    chan = ("zh", "x", "zl")
     return jax.shard_map(
         functools.partial(shards, n_tm, n_chan // NEAR),
         mesh=split,

time: 48.1 us -> 48.2 us (level)
  waiting for transfers between devices: 13.5 us -> 15.4 us
  starting transfers between devices: 15.1 us -> 13.3 us
    ppermute x1 -> x0, starting transfers between devices: 2.63 us -> none  [shards(): far_x = lax.ppermute(near, ('zl', 'x'), [(i, i ^ 3) for i in range(NEAR)])]
    ppermute x9 -> x10, waiting for transfers between devices: 13.5 us -> 15.4 us  [swap(): return lax.ppermute(value, axis, [(i, i ^ distance) for i in range(size)])]
    ppermute x9 -> x10, starting transfers between devices: 6.1 us -> 7.01 us  [swap(): return lax.ppermute(value, axis, [(i, i ^ distance) for i in range(size)])]
where the time goes in v1:
time: 48.2 us; the launch traced here: 47.9 us
  Pallas kernels  16.6 us (34%)
  waiting for transfers between devices  15.4 us (32%)
  starting transfers between devices  13.3 us (28%)
  local copies, waits for them, and re-layouts  2.4 us (5%)
    ppermute x10, waiting for transfers between devices, swap(): return lax.ppermute(value, axis, [(i, i ^ distance) for i in range(size)])  15.4 us
    pallas_call x2, Pallas kernels, correlate(): pl.pallas_call(functools.partial(correlate_kernel, n_parts, flip, first,...  12.2 us
    ppermute x10, starting transfers between devices, swap(): return lax.ppermute(value, axis, [(i, i ^ distance) for i in range(size)])  7.01 us
    all_to_all x1, starting transfers between devices, shards(): got = lax.all_to_all(sent, ('tm', 'x', 'zl'), 0, 0)  6.33 us
    pallas_call x1, Pallas kernels, extract(): pl.pallas_call(functools.partial(extract_kernel, chans // SRC), out_shape...  2.42 us
    unnamed x6, local copies, waits for them, and re-layouts  2.4 us
    pallas_call x1, Pallas kernels, prepare_here(): pl.pallas_call(prepare_here_kernel, out_shape=(full, full, bare, jax.Shap...  1.2 us
  transfers between devices with their start and end apart: 11, of which 3 were waited for; matrix products, arithmetic and copies ran while one was open for 0% of the time, Pallas kernels for 16%

profile of v1, /device:TPU:0, one launch (start us, length us, event | category | flops | bytes accessed | tf_op | source)
XLA Modules:
  0.0 47.9 jit_solution(4454065243670975040)
XLA Ops:
  0.0 2.4 %extract.1 = (bf16[16,24,512]{2,1,0:T(8,128)(2,1)}, s32[3,8,128]{2,1,0:T(8,128)}, bf16[128,1024]{1,0:T(8,128)(2,1)}) custom-call(s32[3]{0:T(128)} %blocks_hbm.1, bf16[2,128,1024]{2,1,0:T(8,128)(2,1)} %traces_ref.3), custom_call_target="tpu_custom_call" | custom-call | tf_op jit(solution)/shard_map/extract/pallas_call | solution.py:78
  2.4 6.3 %all-to-all-start = ((bf16[16,24,512]{2,1,0:T(8,128)(2,1)}), bf16[16,24,512]{2,1,0:T(8,128)(2,1)S(1)}, u32[]{:S(2)}, u32[]{:S(2)}) async-start(bf16[16,24,512]{2,1,0:T(8,128)(2,1)} %get-tuple-element.20), calls=%async_computation | async-start | bytes 786432 | tf_op jit(solution)/shard_map/all_to_all | solution.py:421
  8.8 1.9 %collective-permute-start.8 = (bf16[128,1024]{1,0:T(8,128)(2,1)}, bf16[128,1024]{1,0:T(8,128)(2,1)S(1)}, u32[]{:S(2)}, u32[]{:S(2)}) collective-permute-start(bf16[128,1024]{1,0:T(8,128)(2,1)} %get-tuple-element.24), channel_id=1, source_target_pairs={{0,16},{8,24},{16,0},{24,8},{1,17},{9,25},{17,1},{25,9},{2,18},{10... | collective-permute-start | bytes 786440 | tf_op jit(solution)/shard_map/ppermute | solution.py:414
  10.7 0.0 copy-start
  10.7 1.0 %copy-done = bf16[2,128,1024]{2,1,0:T(8,128)(2,1)S(1)} copy-done((bf16[2,128,1024]{2,1,0:T(8,128)(2,1)S(1)}, bf16[2,128,1024]{2,1,0:T(8,128)(2,1)}, u32[]{:S(2)}) %copy-start) | copy-done | bytes 524312
  11.7 0.0 copy-start.1
  11.7 0.7 %copy-done.1 = s32[3,8,128]{2,1,0:T(8,128)S(1)} copy-done((s32[3,8,128]{2,1,0:T(8,128)S(1)}, s32[3,8,128]{2,1,0:T(8,128)}, u32[]{:S(2)}) %copy-start.1) | copy-done | bytes 12312
  12.4 0.0 copy-start.2
  12.4 0.7 %copy-done.2 = s32[8]{0:T(128)S(1)} copy-done((s32[8]{0:T(128)S(1)}, s32[8]{0:T(128)}, u32[]{:S(2)}) %copy-start.2) | copy-done | bytes 56
  13.1 1.2 %prepare_here.1 = (bf16[3,640,128]{2,1,0:T(8,128)(2,1)S(1)}, bf16[3,640,128]{2,1,0:T(8,128)(2,1)S(1)}, bf16[2,512,128]{2,1,0:T(8,128)(2,1)S(1)}, s32[3,8,128]{2,...) custom-call(s32[8]{0:T(128)S(1)} %copy-done.2, bf16[2,128,1024]{2,1,0:T(8,128)(2,1)S(1)} %copy-done, ...), custom_call_target="tpu_custom_call" | custom-call | bytes 4194304 | tf_op jit(solution)/shard_map/prepare_here/pallas_call | solution.py:215
  14.3 0.1 collective-permute-start.7
  14.4 0.2 collective-permute-start.5
  14.6 7.6 %collective-permute-done.8.refs_0_ = bf16[128,1024]{1,0:T(8,128)(2,1)S(1)} collective-permute-done((bf16[128,1024]{1,0:T(8,128)(2,1)}, bf16[128,1024]{1,0:T(8,128)(2,1)S(1)}, u32[]{:S(2)}, u32[]{:S(2)}) %collective-permute-start.8) | collective-permute-done | bytes 262176 | tf_op jit(solution)/shard_map/ppermute | solution.py:414
  22.3 0.0 collective-permute-start.9
  22.3 0.0 all-to-all-done.got_ref
  22.3 0.2 pick.1.held_ref
  22.5 2.7 %collective-permute-start = (bf16[4,24,512]{2,1,0:T(8,128)(2,1)S(1)}, bf16[4,24,512]{2,1,0:T(8,128)(2,1)S(1)}, u32[]{:S(2)}, u32[]{:S(2)}) collective-permute-start(bf16[4,24,512]{2,1,0:T(8,128)(2,1)S(1)} %pick.1.held_ref), channel_id=1, source_target_pairs={{0,4},{4,0},{1,5},{5,1},{2,6},{6,2},{3,7},{7,3},{8,12},{12,8},{9,1... | collective-permute-start | bytes 294920 | tf_op jit(solution)/shard_map/ppermute | solution.py:414
  25.1 0.2 collective-permute-start.4
  25.4 5.4 %collective-permute-done.came_ref = bf16[4,24,512]{2,1,0:T(8,128)(2,1)S(1)} collective-permute-done((bf16[4,24,512]{2,1,0:T(8,128)(2,1)S(1)}, bf16[4,24,512]{2,1,0:T(8,128)(2,1)S(1)}, u32[]{:S(2)}, u32[]{:S(2)}) %collective-permute-start) | collective-permute-done | bytes 98336 | tf_op jit(solution)/shard_map/ppermute | solution.py:414
  30.8 1.3 %collective-permute-start.2 = (bf16[4,24,512]{2,1,0:T(8,128)(2,1)S(1)}, bf16[4,24,512]{2,1,0:T(8,128)(2,1)S(1)}, u32[]{:S(2)}, u32[]{:S(2)}) collective-permute-start(bf16[4,24,512]{2,1,0:T(8,128)(2,1)S(1)} %choose.1.near_ref), channel_id=1, source_target_pairs={{0,1},{1,0},{2,3},{3,2},{4,5},{5,4},{6,7},{7,6},{8,9},{9,8},{10,11... | collective-permute-start | bytes 294920 | tf_op jit(solution)/shard_map/ppermute | solution.py:414
  32.1 0.0 collective-permute-done.5.refs_2_
  32.1 0.0 collective-permute-start.6
  32.1 0.0 collective-permute-done.9.refs_1_
  32.1 0.6 %prepare_there.1 = (bf16[3,640,128]{2,1,0:T(8,128)(2,1)S(1)}, bf16[3,640,128]{2,1,0:T(8,128)(2,1)S(1)}) custom-call(s32[8,128]{1,0:T(8,128)S(1)} %get-tuple-element.17.count_ref, bf16[128,1024]{1,0:T(8,128)(2,1)S(1)} %collective-permute-done.8.refs_0_, bf16[128,1024]{1,0:T(8,128)(2,1)S(1)} %collective-permute-done.9.refs_1_), custom_call_target="tpu_custom_call" | custom-call | bytes 4194304 | tf_op jit(solution)/shard_map/prepare_there/pallas_call | solution.py:246
  32.8 0.4 collective-permute-start.1
  33.2 2.3 %collective-permute-done.2.far_ref = bf16[4,24,512]{2,1,0:T(8,128)(2,1)S(1)} collective-permute-done((bf16[4,24,512]{2,1,0:T(8,128)(2,1)S(1)}, bf16[4,24,512]{2,1,0:T(8,128)(2,1)S(1)}, u32[]{:S(2)}, u32[]{:S(2)}) %collective-permute-start.2) | collective-permute-done | bytes 98336 | tf_op jit(solution)/shard_map/ppermute | solution.py:414
  35.5 0.2 collective-permute-start.3
  35.6 0.0 collective-permute-done.7.refs_1_
  35.7 5.6 %correlate.2.refs_4_ = f32[3,2,384,512]{3,2,1,0:T(8,128)S(1)} custom-call(s32[8,128]{1,0:T(8,128)S(1)} %get-tuple-element.17.count_ref, bf16[4,24,512]{2,1,0:T(8,128)(2,1)S(1)} %choose.1.near_ref, bf16[4,24,512]{2,1,0:T(8,128)(2,1)S(1)} %collective-permute-done.2.far_ref, bf16[3,640,128]{2,1,0:T(8,128)(2,1)S(1)} %get-tuple-element.23.refs_0_, ...), custom_call_target="tpu_custom_call" | custom-call | flops 3812622336 | bytes 8388608 | tf_op jit(solution)/shard_map/correlate/pallas_call | solution.py:399
  41.2 0.0 collective-permute-done.4.refs_1_
  41.2 0.0 collective-permute-done.6.refs_3_
  41.3 0.0 collective-permute-done.1.near_ref
  41.3 0.0 collective-permute-done.3.far_ref
  41.3 6.6 %correlate.3 = f32[3,201,8,128]{3,2,1,0:T(8,128)} custom-call(s32[8,128]{1,0:T(8,128)S(1)} %get-tuple-element.17.count_ref, bf16[4,24,512]{2,1,0:T(8,128)(2,1)S(1)} %collective-permute-done.1.near_ref, bf16[4,24,512]{2,1,0:T(8,128)(2,1)S(1)} %collective-permute-done.3.far_ref, bf16[3,640,128]{2,1,0:T(8,128)(2,1)S(1)} %get-tuple-element.21.refs_0_, ...), custom_call_target="tpu_custom_call" | custom-call | flops 3812622336 | bytes 8388608 | tf_op jit(solution)/shard_map/correlate/pallas_call | solution.py:399
  (1 shorter events, 0.0 us)
Async XLA Ops:
  2.4 19.8 %all-to-all-start = ((bf16[16,24,512]{2,1,0:T(8,128)(2,1)}), bf16[16,24,512]{2,1,0:T(8,128)(2,1)S(1)}, u32[]{:S(2)}, u32[]{:S(2)}) async-start(bf16[16,24,512]{2,1,0:T(8,128)(2,1)} %get-tuple-element.20), calls=%async_computation | async-start | bytes 786432 | tf_op jit(solution)/shard_map/all_to_all | solution.py:421
  8.8 13.5 %collective-permute-start.8 = (bf16[128,1024]{1,0:T(8,128)(2,1)}, bf16[128,1024]{1,0:T(8,128)(2,1)S(1)}, u32[]{:S(2)}, u32[]{:S(2)}) collective-permute-start(bf16[128,1024]{1,0:T(8,128)(2,1)} %get-tuple-element.24), channel_id=1, source_target_pairs={{0,16},{8,24},{16,0},{24,8},{1,17},{9,25},{17,1},{25,9},{2,18},{10... | collective-permute-start | bytes 786440 | tf_op jit(solution)/shard_map/ppermute | solution.py:414
  10.7 1.0 %copy-start = (bf16[2,128,1024]{2,1,0:T(8,128)(2,1)S(1)}, bf16[2,128,1024]{2,1,0:T(8,128)(2,1)}, u32[]{:S(2)}) copy-start(bf16[2,128,1024]{2,1,0:T(8,128)(2,1)} %traces_ref.3) | copy-start | bytes 1572868
  11.7 0.7 %copy-start.1 = (s32[3,8,128]{2,1,0:T(8,128)S(1)}, s32[3,8,128]{2,1,0:T(8,128)}, u32[]{:S(2)}) copy-start(s32[3,8,128]{2,1,0:T(8,128)} %get-tuple-element.16.owner_ref) | copy-start | bytes 36868
  12.4 0.7 %copy-start.2 = (s32[8]{0:T(128)S(1)}, s32[8]{0:T(128)}, u32[]{:S(2)}) copy-start(s32[8]{0:T(128)} %len_ref.1) | copy-start | bytes 100
  14.3 21.3 %collective-permute-start.7 = (bf16[3,640,128]{2,1,0:T(8,128)(2,1)S(1)}, bf16[3,640,128]{2,1,0:T(8,128)(2,1)S(1)}, u32[]{:S(2)}, u32[]{:S(2)}) collective-permute-start(bf16[3,640,128]{2,1,0:T(8,128)(2,1)S(1)} %get-tuple-element.23.refs_0_), channel_id=1, source_target_pairs={{0,8},{8,0},{16,24},{24,16},{1,9},{9,1},{17,25},{25,17},{2,10},{10... | collective-permute-start | bytes 1474568 | tf_op jit(solution)/shard_map/ppermute | solution.py:414
  14.4 17.8 %collective-permute-start.5 = (bf16[2,512,128]{2,1,0:T(8,128)(2,1)S(1)}, bf16[2,512,128]{2,1,0:T(8,128)(2,1)S(1)}, u32[]{:S(2)}, u32[]{:S(2)}) collective-permute-start(bf16[2,512,128]{2,1,0:T(8,128)(2,1)S(1)} %get-tuple-element.22), channel_id=1, source_target_pairs={{0,16},{8,24},{16,0},{24,8},{1,17},{9,25},{17,1},{25,9},{2,18},{10... | collective-permute-start | bytes 786440 | tf_op jit(solution)/shard_map/ppermute | solution.py:414
  22.3 9.9 %collective-permute-start.9 = (bf16[128,1024]{1,0:T(8,128)(2,1)S(1)}, bf16[128,1024]{1,0:T(8,128)(2,1)S(1)}, u32[]{:S(2)}, u32[]{:S(2)}) collective-permute-start(bf16[128,1024]{1,0:T(8,128)(2,1)S(1)} %collective-permute-done.8.refs_0_), channel_id=1, source_target_pairs={{0,8},{8,0},{16,24},{24,16},{1,9},{9,1},{17,25},{25,17},{2,10},{10... | collective-permute-start | bytes 786440 | tf_op jit(solution)/shard_map/ppermute | solution.py:414
  22.5 8.3 %collective-permute-start = (bf16[4,24,512]{2,1,0:T(8,128)(2,1)S(1)}, bf16[4,24,512]{2,1,0:T(8,128)(2,1)S(1)}, u32[]{:S(2)}, u32[]{:S(2)}) collective-permute-start(bf16[4,24,512]{2,1,0:T(8,128)(2,1)S(1)} %pick.1.held_ref), channel_id=1, source_target_pairs={{0,4},{4,0},{1,5},{5,1},{2,6},{6,2},{3,7},{7,3},{8,12},{12,8},{9,1... | collective-permute-start | bytes 294920 | tf_op jit(solution)/shard_map/ppermute | solution.py:414
  25.1 16.1 %collective-permute-start.4 = (bf16[3,640,128]{2,1,0:T(8,128)(2,1)S(1)}, bf16[3,640,128]{2,1,0:T(8,128)(2,1)S(1)}, u32[]{:S(2)}, u32[]{:S(2)}) collective-permute-start(bf16[3,640,128]{2,1,0:T(8,128)(2,1)S(1)} %get-tuple-element.21.refs_0_), channel_id=1, source_target_pairs={{0,8},{8,0},{16,24},{24,16},{1,9},{9,1},{17,25},{25,17},{2,10},{10... | collective-permute-start | bytes 1474568 | tf_op jit(solution)/shard_map/ppermute | solution.py:414
  30.8 4.7 %collective-permute-start.2 = (bf16[4,24,512]{2,1,0:T(8,128)(2,1)S(1)}, bf16[4,24,512]{2,1,0:T(8,128)(2,1)S(1)}, u32[]{:S(2)}, u32[]{:S(2)}) collective-permute-start(bf16[4,24,512]{2,1,0:T(8,128)(2,1)S(1)} %choose.1.near_ref), channel_id=1, source_target_pairs={{0,1},{1,0},{2,3},{3,2},{4,5},{5,4},{6,7},{7,6},{8,9},{9,8},{10,11... | collective-permute-start | bytes 294920 | tf_op jit(solution)/shard_map/ppermute | solution.py:414
  32.1 9.1 %collective-permute-start.6 = (bf16[2,512,128]{2,1,0:T(8,128)(2,1)S(1)}, bf16[2,512,128]{2,1,0:T(8,128)(2,1)S(1)}, u32[]{:S(2)}, u32[]{:S(2)}) collective-permute-start(bf16[2,512,128]{2,1,0:T(8,128)(2,1)S(1)} %collective-permute-done.5.refs_2_), channel_id=1, source_target_pairs={{0,8},{8,0},{16,24},{24,16},{1,9},{9,1},{17,25},{25,17},{2,10},{10... | collective-permute-start | bytes 786440 | tf_op jit(solution)/shard_map/ppermute | solution.py:414
  32.8 8.5 %collective-permute-start.1 = (bf16[4,24,512]{2,1,0:T(8,128)(2,1)S(1)}, bf16[4,24,512]{2,1,0:T(8,128)(2,1)S(1)}, u32[]{:S(2)}, u32[]{:S(2)}) collective-permute-start(bf16[4,24,512]{2,1,0:T(8,128)(2,1)S(1)} %choose.1.near_ref), channel_id=1, source_target_pairs={{0,2},{2,0},{1,3},{3,1},{4,6},{6,4},{5,7},{7,5},{8,10},{10,8},{9,1... | collective-permute-start | bytes 294920 | tf_op jit(solution)/shard_map/ppermute | solution.py:414
  35.5 5.8 %collective-permute-start.3 = (bf16[4,24,512]{2,1,0:T(8,128)(2,1)S(1)}, bf16[4,24,512]{2,1,0:T(8,128)(2,1)S(1)}, u32[]{:S(2)}, u32[]{:S(2)}) collective-permute-start(bf16[4,24,512]{2,1,0:T(8,128)(2,1)S(1)} %collective-permute-done.2.far_ref), channel_id=1, source_target_pairs={{0,2},{2,0},{1,3},{3,1},{4,6},{6,4},{5,7},{7,5},{8,10},{10,8},{9,1... | collective-permute-start | bytes 294920 | tf_op jit(solution)/shard_map/ppermute | solution.py:414
